TPU v7x, 32 devices: a whole 2x2x4 slice. The times are simulated.
32 devices in a mesh: grp: 8 (over z, y), mem: 4 (over x, core).
Axes of the slice: x: 2, y: 2, z: 4, core: 2. Of those that a mesh axis runs over, the one named last changes fastest.
Arguments:
- codes: bfloat16 [8192, 1024], P(('grp', 'mem')), as said below
- scales: float32 [8192, 8], P(('grp', 'mem')), may hold values from 0.2 to 2
- cluster_id: int32 [8192], P(('grp', 'mem')), may hold values from 0 to 63, as said below
Outputs:
- smoothed: bfloat16 [8192, 1024], P(('grp', 'mem'))
- dup_mass: bfloat16 [8192], P(('grp', 'mem'))
Inputs may be any that keep to these rules, and one draw needn't show every extreme that they name: `cluster_id`: cluster c belongs to owner group c mod 8. Among the 256 documents of one device, at most 40 belong to clusters of any one owner group, and at most 20 to any one cluster; for each index along mem, some owner group gets exactly 40 from every device of that index, and some cluster of that group exactly 20 from every device of that index. `codes`: documents of one cluster lie near a common direction.
All inputs are finite; a program needn't handle non-finite values.
Results may differ from a plain program's by a relative error of at most 0.0034.
Values may be sent and summed in bfloat16 or wider, within the bound.
No kernel may reach another device: no remote copies, remote signals or barrier semaphores. Data moves between devices by JAX's collectives and lax.ppermute only.
A program may use at most 64 MiB of HBM per device.

v0:
```python
import jax
import jax.numpy as jnp
from jax import lax
from jax.sharding import PartitionSpec as P

CAP = 40


def embed(codes, scales):
    rows, width = codes.shape
    nblk = scales.shape[1]
    x = (codes.astype(jnp.float32).reshape(rows, nblk, width // nblk) * scales[:, :, None]).reshape(
        rows, width
    )
    inv = lax.rsqrt(jnp.mean(x * x, axis=1, keepdims=True) + 1e-06)
    return (x * inv).astype(jnp.bfloat16)


def make_fold(queries, qtags, query_index):
    width = queries.shape[1]

    def accumulate(carry, piece, start):
        keys, ktags = piece
        member_count = keys.shape[0]
        sims = (
            lax.dot_general(
                queries, keys, (((1,), (1,)), ((), ())), preferred_element_type=jnp.float32
            )
            / width
        )
        key_index = jnp.arange(member_count, dtype=jnp.int32)
        keep = (
            (qtags[:, None] == ktags[None, :])
            & (qtags[:, None] >= 0)
            & (query_index[:, None] != key_index[None, :])
        )
        weights = jnp.where(keep, jnp.exp(8.0 * (sims - 1.0)), jnp.float32(0.0))
        den_sum = jnp.sum(weights, axis=1)
        numerator_sum = jnp.dot(
            weights.astype(jnp.bfloat16), keys, preferred_element_type=jnp.float32
        )
        return (den_sum, numerator_sum)

    return accumulate


def local(codes, scales, cluster_id):
    rows, width = codes.shape
    groups = lax.axis_size("grp")
    member = lax.axis_index("mem")
    embedding_rows = embed(codes, scales)
    owner = cluster_id % groups
    onehot = (owner[:, None] == jnp.arange(groups, dtype=jnp.int32)[None, :]).astype(jnp.int32)
    ranks = jnp.cumsum(onehot, axis=0) - 1
    slot = jnp.sum(ranks * onehot, axis=1)
    target = owner * CAP + slot
    outbox = (
        jnp.zeros((groups * CAP, width), jnp.bfloat16)
        .at[target]
        .set(embedding_rows)
        .reshape(groups, CAP, width)
    )
    outtags = (
        jnp.full((groups * CAP,), -1.0, jnp.float32)
        .at[target]
        .set(cluster_id.astype(jnp.float32))
        .astype(jnp.bfloat16)
        .reshape(groups, CAP)
    )
    slots = groups * CAP
    inbox, incoming_tags = (
        lax.all_to_all(outbox, "grp", split_axis=0, concat_axis=0, tiled=True),
        lax.all_to_all(outtags, "grp", split_axis=0, concat_axis=0, tiled=True),
    )
    queries = inbox.reshape(slots, width)
    qtags = incoming_tags.reshape(slots)
    start_carry = (jnp.zeros((slots,), jnp.float32), jnp.zeros((slots, width), jnp.float32))
    query_index = member * slots + jnp.arange(slots, dtype=jnp.int32)
    accumulate = make_fold(queries, qtags, query_index)
    den_sum, numerator_sum = accumulate(
        start_carry,
        (
            lax.all_gather(queries, "mem", axis=0, tiled=True),
            lax.all_gather(qtags, "mem", axis=0, tiled=True),
        ),
        jnp.int32(0),
    )
    den = 1.0 + den_sum
    result = ((queries.astype(jnp.float32) + numerator_sum) / den[:, None]).astype(jnp.bfloat16)
    mass = jnp.log(den).astype(jnp.bfloat16)
    back_rows, back_mass = (
        lax.all_to_all(
            result.reshape(groups, CAP, width), "grp", split_axis=0, concat_axis=0, tiled=True
        ),
        lax.all_to_all(mass.reshape(groups, CAP), "grp", split_axis=0, concat_axis=0, tiled=True),
    )
    smoothed = back_rows.reshape(slots, width)[target]
    dup_mass = back_mass.reshape(slots)[target]
    return (smoothed, dup_mass)


def solution(mesh):
    placed = (P(("grp", "mem"), None), P(("grp", "mem"), None), P(("grp", "mem")))
    return jax.shard_map(
        local,
        mesh=mesh,
        in_specs=placed,
        out_specs=(P(("grp", "mem"), None), P(("grp", "mem"))),
        check_vma=False,
    )
```

profile of v0, /device:TPU:0, one launch (start us, length us, event | category | flops | bytes accessed | tf_op | source)
XLA Modules:
  0.0 107.8 jit_solution(3126384838830802530)
XLA Ops:
  7.2 0.0 copy-start.1
  7.2 0.0 all-gather.2.cloned.1.call-start
  7.2 0.8 fusion.14
  8.0 0.6 reduce-window.6
  8.6 0.2 slice_reduce_fusion
  8.8 0.1 fusion.9
  8.9 0.8 copy.7
  9.8 0.3 mul.43
  10.1 0.0 copy-done.1
  10.1 0.3 multiply_reduce_fusion
  10.4 0.0 copy-start.3
  10.4 2.0 %scatter_custom_fusion = bf16[320,1024]{1,0:T(8,128)(2,1)S(1)} fusion(s32[256]{0:T(256)S(1)} %compare_select_fusion, f32[32,8,8,128]{3,2,1,0:T(8,128)S(1)} %bitcast.26, bf16[256,1024]{1,0:T(8,128)(2,1)S(1)} %copy-done.1, f32[256]{0:T(256)S(1)} %add_rsqrt_fusion, bf16[]{:T(256)} %constant.16.clone.1), kind=kCustom, calls=%fused_computation.17 | custom fusion | flops 1048576 | bytes 2229250 | tf_op jit(solution)/shard_map/scatter | solution.py:60
  12.4 24.9 %all_to_all.26 = bf16[8,40,1024]{2,1,0:T(8,128)(2,1)} all-to-all(bf16[8,40,1024]{2,1,0:T(8,128)(2,1)S(1)} %bitcast.30), channel_id=1, replica_groups=mesh['grp'=8,'mem'=4] {'grp'}, dimensions={0} | all-to-all | bytes 1310720 | tf_op jit(solution)/shard_map/all_to_all | solution.py:72
  37.3 0.0 all-gather.2.cloned.1.call-update
  37.3 1.4 %scatter_custom_fusion.1 = f32[320]{0:T(512)S(1)} fusion(s32[256]{0:T(256)S(1)} %compare_select_fusion, f32[256]{0:T(256)S(1)} %get-tuple-element.4, f32[]{:T(128)} %constant.49.clone.1), kind=kCustom, calls=%fused_computation.35 | custom fusion | bytes 1284 | tf_op jit(solution)/shard_map/scatter | solution.py:66
  38.7 0.7 all_to_all.21
  39.4 3.3 %all-to-all-start.1 = ((bf16[8,1,40]{2,1,0:T(2,128)(2,1)}), bf16[8,1,40]{2,1,0:T(2,128)(2,1)S(1)}, u32[]{:S(2)}, u32[]{:S(2)}) async-start(bf16[8,1,40]{2,1,0:T(2,128)(2,1)} %all_to_all.21), calls=%async_computation.1 | async-start | bytes 8192 | tf_op jit(solution)/shard_map/all_to_all | solution.py:73
  42.8 0.0 copy-done.3
  42.8 0.6 dynamic-slice
  44.0 5.1 %all-to-all-done.1 = bf16[8,1,40]{2,1,0:T(2,128)(2,1)S(1)} async-done(((bf16[8,1,40]{2,1,0:T(2,128)(2,1)}), bf16[8,1,40]{2,1,0:T(2,128)(2,1)S(1)}, u32[]{:S(2)}, u32[]{:S(2)}) %all-to-all-start.1) | async-done | bytes 672 | tf_op jit(solution)/shard_map/all_to_all | solution.py:73
  49.1 0.1 reshape.140
  49.2 0.3 dynamic-update-slice
  49.4 6.1 %all-reduce = bf16[1280]{0:T(1024)(128)(2,1)S(1)} all-reduce(bf16[1280]{0:T(1024)(128)(2,1)S(1)} %dynamic-update-slice), channel_id=1, replica_groups=mesh['grp'=8,'mem'=4] {'mem'}, use_global_device_ids=true, to_apply=%add | all-reduce | flops 1280 | bytes 5120
  55.6 0.0 copy-start
  55.6 6.2 %all-gather.2.cloned.1.call-done = bf16[1280,1024]{1,0:T(8,128)(2,1)} async-done(((bf16[320,1024]{1,0:T(8,128)(2,1)}), bf16[1280,1024]{1,0:T(8,128)(2,1)}) %all-gather.2.cloned.1.call-update) | async-done | bytes 2621456 | tf_op jit(solution)/shard_map/all_gather | solution.py:83
  61.8 0.0 copy-start.2
  61.8 4.5 %fusion.15 = (f32[320]{0:T(512)S(1)}, bf16[320,1280]{1,0:T(8,128)(2,1)}) fusion(bf16[320,1024]{1,0:T(8,128)(2,1)} %bitcast.28, bf16[1280,1024]{1,0:T(8,128)(2,1)} %all-gather.2.cloned.1.call-done, s32[320]{0:T(512)S(1)} %iota_add_fusion, pred[320]{0:T(512)(128)(4,1)S(1)} %broadcast_compare_fusion, bf16[1280]{0:T(1024)(128)(2,1)S(1)} %all-reduce, ...), kind=kOutput, calls=%fused_computation.40 | convolution fusion | flops 843775680 | bytes 4102080 | tf_op jit(solution)/shard_map/dot_general | solution.py:26
  66.3 0.7 convert_element_type.50
  67.0 5.5 %all-to-all-start.3 = ((bf16[8,1,40]{2,1,0:T(2,128)(2,1)}), bf16[8,1,40]{2,1,0:T(2,128)(2,1)S(1)}, u32[]{:S(2)}, u32[]{:S(2)}) async-start(bf16[8,1,40]{2,1,0:T(2,128)(2,1)} %convert_element_type.50), calls=%async_computation.3 | async-start | bytes 8192 | tf_op jit(solution)/shard_map/all_to_all | solution.py:95
  72.5 0.0 copy-done
  72.5 0.0 copy-done.2
  72.5 3.1 %divide_convert_fusion = bf16[320,1024]{1,0:T(8,128)(2,1)} fusion(bf16[1280,1024]{1,0:T(8,128)(2,1)S(1)} %copy-done.2, bf16[320,1024]{1,0:T(8,128)(2,1)S(1)} %bitcast.29, bf16[320,1280]{1,0:T(8,128)(2,1)} %get-tuple-element.7, f32[320]{0:T(512)S(1)} %get-tuple-element.3), kind=kOutput, calls=%fused_computation.12 | convolution fusion | flops 840171520 | bytes 4752640 | tf_op jit(solution)/shard_map/dot_general | solution.py:39
  75.6 3.3 %all-to-all-done.3 = bf16[8,1,40]{2,1,0:T(2,128)(2,1)S(1)} async-done(((bf16[8,1,40]{2,1,0:T(2,128)(2,1)}), bf16[8,1,40]{2,1,0:T(2,128)(2,1)S(1)}, u32[]{:S(2)}, u32[]{:S(2)}) %all-to-all-start.3) | async-done | bytes 672 | tf_op jit(solution)/shard_map/all_to_all | solution.py:95
  78.9 3.5 %all-to-all-start.2 = ((bf16[8,40,1024]{2,1,0:T(8,128)(2,1)}), bf16[8,40,1024]{2,1,0:T(8,128)(2,1)S(1)}, u32[]{:S(2)}, u32[]{:S(2)}) async-start(bf16[8,40,1024]{2,1,0:T(8,128)(2,1)} %bitcast.6), calls=%async_computation.2 | async-start | bytes 1310720 | tf_op jit(solution)/shard_map/all_to_all | solution.py:92
  82.5 0.1 reshape.103
  82.6 2.5 %gather_fusion.1 = bf16[256]{0:T(256)(128)(2,1)} fusion(bf16[320]{0:T(512)(128)(2,1)S(1)} %reshape.103, s32[1024]{0:T(1024)S(1)} %pad_clamp_fusion), kind=kCustom, calls=%fused_computation.1 | custom fusion | bytes 2048 | tf_op jit(solution)/shard_map/gather | solution.py:98
  85.0 13.9 %all-to-all-done.2 = bf16[8,40,1024]{2,1,0:T(8,128)(2,1)S(1)} async-done(((bf16[8,40,1024]{2,1,0:T(8,128)(2,1)}), bf16[8,40,1024]{2,1,0:T(8,128)(2,1)S(1)}, u32[]{:S(2)}, u32[]{:S(2)}) %all-to-all-start.2) | async-done | bytes 655392 | tf_op jit(solution)/shard_map/all_to_all | solution.py:92
  98.9 2.0 %gather_fusion = bf16[256,1024]{1,0:T(8,128)(2,1)} fusion(bf16[320,1024]{1,0:T(8,128)(2,1)S(1)} %bitcast.24, s32[1024]{0:T(1024)S(1)} %pad_clamp_fusion), kind=kCustom, calls=%fused_computation | custom fusion | bytes 1049600 | tf_op jit(solution)/shard_map/gather | solution.py:97
  (13 shorter events, 0.1 us)
Async XLA Ops:
  7.2 2.9 %copy-start.1 = (bf16[256,1024]{1,0:T(8,128)(2,1)S(1)}, bf16[256,1024]{1,0:T(8,128)(2,1)}, u32[]{:S(2)}) copy-start(bf16[256,1024]{1,0:T(8,128)(2,1)} %param.3) | copy-start | bytes 1572868
  7.2 54.6 %all-gather.2.cloned.1.call-start = ((), (), s32[]{:S(2)}) async-start(), calls=%async_computation.4 | async-start | bytes 3276800 | tf_op jit(solution)/shard_map/all_gather | solution.py:83
  10.4 32.4 %copy-start.3 = (u32[32]{0:T(128)S(1)}, u32[32]{0:T(128)}, u32[]{:S(2)}) copy-start(u32[32]{0:T(128)} %constant.55) | copy-start | bytes 388
  39.4 9.6 %all-to-all-start.1 = ((bf16[8,1,40]{2,1,0:T(2,128)(2,1)}), bf16[8,1,40]{2,1,0:T(2,128)(2,1)S(1)}, u32[]{:S(2)}, u32[]{:S(2)}) async-start(bf16[8,1,40]{2,1,0:T(2,128)(2,1)} %all_to_all.21), calls=%async_computation.1 | async-start | bytes 8192 | tf_op jit(solution)/shard_map/all_to_all | solution.py:73
  55.6 16.9 %copy-start = (bf16[8,40,1024]{2,1,0:T(8,128)(2,1)S(1)}, bf16[8,40,1024]{2,1,0:T(8,128)(2,1)}, u32[]{:S(2)}) copy-start(bf16[8,40,1024]{2,1,0:T(8,128)(2,1)} %all_to_all.26) | copy-start | bytes 1966084
  61.8 10.7 %copy-start.2 = (bf16[1280,1024]{1,0:T(8,128)(2,1)S(1)}, bf16[1280,1024]{1,0:T(8,128)(2,1)}, u32[]{:S(2)}) copy-start(bf16[1280,1024]{1,0:T(8,128)(2,1)} %all-gather.2.cloned.1.call-done) | copy-start | bytes 7864324
  67.0 11.9 %all-to-all-start.3 = ((bf16[8,1,40]{2,1,0:T(2,128)(2,1)}), bf16[8,1,40]{2,1,0:T(2,128)(2,1)S(1)}, u32[]{:S(2)}, u32[]{:S(2)}) async-start(bf16[8,1,40]{2,1,0:T(2,128)(2,1)} %convert_element_type.50), calls=%async_computation.3 | async-start | bytes 8192 | tf_op jit(solution)/shard_map/all_to_all | solution.py:95
  78.9 20.1 %all-to-all-start.2 = ((bf16[8,40,1024]{2,1,0:T(8,128)(2,1)}), bf16[8,40,1024]{2,1,0:T(8,128)(2,1)S(1)}, u32[]{:S(2)}, u32[]{:S(2)}) async-start(bf16[8,40,1024]{2,1,0:T(8,128)(2,1)} %bitcast.6), calls=%async_computation.2 | async-start | bytes 1310720 | tf_op jit(solution)/shard_map/all_to_all | solution.py:92
Sparse Core Ops, SparseCore 0:
  37.4 24.3 all-gather.1
where the time goes:
time: 108 us
  blocking collectives  31 us (29%)
  waiting for transfers between devices  28.5 us (26%)
  between operations  14.8 us (14%)
  starting transfers between devices  12.4 us (11%)
  local copies, waits for them, and re-layouts  9.58 us (9%)
  matrix products  7.54 us (7%)
  other arithmetic  3.82 us (4%)
    all_to_all x1, blocking collectives, local(): lax.all_to_all(outbox, 'grp', split_axis=0, concat_axis=0, tiled=True)  24.9 us
    all_to_all x1, waiting for transfers between devices, local(): lax.all_to_all(result.reshape(groups, CAP, width), 'grp', split_axis=0, c...  13.9 us
    all_gather x1, waiting for transfers between devices, local(): lax.all_gather(queries, 'mem', axis=0, tiled=True)  6.2 us
    unnamed x1, blocking collectives  6.14 us
    all_to_all x1, starting transfers between devices, local(): lax.all_to_all(mass.reshape(groups, CAP), 'grp', split_axis=0, concat_axi...  5.52 us
    all_to_all x1, waiting for transfers between devices, local(): lax.all_to_all(outtags, 'grp', split_axis=0, concat_axis=0, tiled=True)  5.05 us
    dot_general x1, matrix products, accumulate(): lax.dot_general(queries, keys, (((1,), (1,)), ((), ())), preferred_elemen...  4.49 us
    all_to_all x1, starting transfers between devices, local(): lax.all_to_all(result.reshape(groups, CAP, width), 'grp', split_axis=0, c...  3.54 us
  transfers between devices with their start and end apart: 4, of which 4 were waited for; matrix products, arithmetic and copies ran while one was open for 7% of the time, Pallas kernels for 0%

commit v1 on v0

--- a/solution.py
+++ b/solution.py
@@ -2,6 +2,7 @@
 import jax.numpy as jnp
 from jax import lax
 from jax.sharding import PartitionSpec as P
+from jax.lax import axis_index, axis_size, ppermute
 
 CAP = 40
 
@@ -88,10 +89,24 @@
     den = 1.0 + den_sum
     result = ((queries.astype(jnp.float32) + numerator_sum) / den[:, None]).astype(jnp.bfloat16)
     mass = jnp.log(den).astype(jnp.bfloat16)
+
+    def surface_carry(content, group_axis):
+        u1 = axis_size(group_axis)
+        local_out = axis_index(group_axis)
+        p_next, plain = (u1, local_out)
+        heard = content.shape[0] // p_next
+        raw_out = jnp.roll(content, shift=-plain * heard, axis=0)
+        block_next = lax.slice_in_dim(raw_out, 0, heard, axis=0)
+        fields = [block_next]
+        for s in tuple(range(1, p_next)):
+            r_now = lax.slice_in_dim(raw_out, s * heard, (s + 1) * heard, axis=0)
+            prior = ppermute(r_now, group_axis, [(at, (at + s) % p_next) for at in range(p_next)])
+            fields.append(prior)
+        odd = jnp.concatenate(fields[::-1], axis=0)
+        return jnp.roll(odd, (plain + 1) * fields[0].shape[0], axis=0)
+
     back_rows, back_mass = (
-        lax.all_to_all(
-            result.reshape(groups, CAP, width), "grp", split_axis=0, concat_axis=0, tiled=True
-        ),
+        surface_carry(result.reshape(groups, CAP, width), "grp"),
         lax.all_to_all(mass.reshape(groups, CAP), "grp", split_axis=0, concat_axis=0, tiled=True),
     )
     smoothed = back_rows.reshape(slots, width)[target]

time: 108 us -> 103 us (0.954)
  waiting for transfers between devices: 28.5 us -> 17.1 us
  starting transfers between devices: 12.4 us -> 21.1 us
  matrix products: 7.54 us -> 4.72 us
    ppermute x0 -> x7, starting transfers between devices: none -> 14.5 us  [surface_carry(): ppermute(r_now, group_axis, [(at, (at + s) % p_next) for at in range(p_ne...]
    all_to_all x1 -> x0, waiting for transfers between devices: 13.9 us -> none  [local(): lax.all_to_all(result.reshape(groups, CAP, width), 'grp', split_axis=0, c...]
    ppermute x0 -> x7, waiting for transfers between devices: none -> 5.84 us  [surface_carry(): ppermute(r_now, group_axis, [(at, (at + s) % p_next) for at in range(p_ne...]
    all_to_all x1 -> x0, starting transfers between devices: 3.54 us -> none  [local(): lax.all_to_all(result.reshape(groups, CAP, width), 'grp', split_axis=0, c...]
    all_to_all x1, waiting for transfers between devices: 3.32 us -> 0.01 us  [local(): lax.all_to_all(mass.reshape(groups, CAP), 'grp', split_axis=0, concat_axi...]
    all_to_all x1, starting transfers between devices: 5.52 us -> 3.31 us  [local(): lax.all_to_all(mass.reshape(groups, CAP), 'grp', split_axis=0, concat_axi...]
    dot_general x1, matrix products: 3.05 us -> 1.04 us  [accumulate(): jnp.dot(weights.astype(jnp.bfloat16), keys, preferred_element_type=jnp.fl...]
  transfers between devices with their start and end apart: 4 -> 10, of which waited for: 4 -> 4; matrix products, arithmetic and copies ran while one was open for 7% -> 5% of each run, Pallas kernels for 0% -> 0%
where the time goes in v1:
time: 103 us
  blocking collectives  31 us (30%)
  starting transfers between devices  21.1 us (20%)
  waiting for transfers between devices  17.1 us (17%)
  between operations  15 us (15%)
  local copies, waits for them, and re-layouts  9.67 us (9%)
  matrix products  4.72 us (5%)
  other arithmetic  4.33 us (4%)
    all_to_all x1, blocking collectives, local(): lax.all_to_all(outbox, 'grp', split_axis=0, concat_axis=0, tiled=True)  24.9 us
    ppermute x7, starting transfers between devices, surface_carry(): ppermute(r_now, group_axis, [(at, (at + s) % p_next) for at in range(p_ne...  14.5 us
    all_gather x1, waiting for transfers between devices, local(): lax.all_gather(queries, 'mem', axis=0, tiled=True)  6.2 us
    unnamed x1, blocking collectives  6.14 us
    ppermute x7, waiting for transfers between devices, surface_carry(): ppermute(r_now, group_axis, [(at, (at + s) % p_next) for at in range(p_ne...  5.84 us
    all_to_all x1, waiting for transfers between devices, local(): lax.all_to_all(outtags, 'grp', split_axis=0, concat_axis=0, tiled=True)  5.02 us
    dot_general x1, matrix products, accumulate(): lax.dot_general(queries, keys, (((1,), (1,)), ((), ())), preferred_elemen...  3.68 us
    all_to_all x1, starting transfers between devices, local(): lax.all_to_all(outtags, 'grp', split_axis=0, concat_axis=0, tiled=True)  3.31 us
  transfers between devices with their start and end apart: 10, of which 4 were waited for; matrix products, arithmetic and copies ran while one was open for 5% of the time, Pallas kernels for 0%

profile of v1, /device:TPU:0, one launch (start us, length us, event | category | flops | bytes accessed | tf_op | source)
XLA Modules:
  0.0 103.0 jit_solution(16545108151875446343)
XLA Ops:
  7.2 0.0 copy-start.1
  7.2 0.0 all-gather.2.cloned.1.call-start
  7.2 0.8 fusion.17
  8.0 0.6 reduce-window.6
  8.6 0.2 slice_reduce_fusion
  8.8 0.1 fusion.11
  8.9 0.8 copy.7
  9.8 0.3 mul.43
  10.1 0.0 copy-done.1
  10.1 0.3 multiply_reduce_fusion
  10.4 0.0 copy-start.3
  10.4 2.0 %scatter_custom_fusion = bf16[320,1024]{1,0:T(8,128)(2,1)S(1)} fusion(s32[256]{0:T(256)S(1)} %compare_select_fusion, f32[32,8,8,128]{3,2,1,0:T(8,128)S(1)} %bitcast.26, bf16[256,1024]{1,0:T(8,128)(2,1)S(1)} %copy-done.1, f32[256]{0:T(256)S(1)} %add_rsqrt_fusion, bf16[]{:T(256)} %constant.60.clone.1), kind=kCustom, calls=%fused_computation.23 | custom fusion | flops 1048576 | bytes 2229250 | tf_op jit(solution)/shard_map/scatter | solution.py:61
  12.4 24.9 %all_to_all.21 = bf16[8,40,1024]{2,1,0:T(8,128)(2,1)} all-to-all(bf16[8,40,1024]{2,1,0:T(8,128)(2,1)S(1)} %bitcast.30), channel_id=1, replica_groups=mesh['grp'=8,'mem'=4] {'grp'}, dimensions={0} | all-to-all | bytes 1310720 | tf_op jit(solution)/shard_map/all_to_all | solution.py:73
  37.3 0.0 all-gather.2.cloned.1.call-update
  37.3 1.4 %scatter_custom_fusion.1 = f32[320]{0:T(512)S(1)} fusion(s32[256]{0:T(256)S(1)} %compare_select_fusion, f32[256]{0:T(256)S(1)} %get-tuple-element.12, f32[]{:T(128)} %constant.70.clone.1), kind=kCustom, calls=%fused_computation.49 | custom fusion | bytes 1284 | tf_op jit(solution)/shard_map/scatter | solution.py:67
  38.7 0.7 all_to_all.17
  39.4 3.3 %all-to-all-start.1 = ((bf16[8,1,40]{2,1,0:T(2,128)(2,1)}), bf16[8,1,40]{2,1,0:T(2,128)(2,1)S(1)}, u32[]{:S(2)}, u32[]{:S(2)}) async-start(bf16[8,1,40]{2,1,0:T(2,128)(2,1)} %all_to_all.17), calls=%async_computation.1 | async-start | bytes 8192 | tf_op jit(solution)/shard_map/all_to_all | solution.py:74
  42.8 0.0 copy-done.3
  42.8 0.6 dynamic-slice
  44.0 5.0 %all-to-all-done.1 = bf16[8,1,40]{2,1,0:T(2,128)(2,1)S(1)} async-done(((bf16[8,1,40]{2,1,0:T(2,128)(2,1)}), bf16[8,1,40]{2,1,0:T(2,128)(2,1)S(1)}, u32[]{:S(2)}, u32[]{:S(2)}) %all-to-all-start.1) | async-done | bytes 672 | tf_op jit(solution)/shard_map/all_to_all | solution.py:74
  49.1 0.1 reshape.140
  49.2 0.3 dynamic-update-slice
  49.4 6.1 %all-reduce = bf16[1280]{0:T(1024)(128)(2,1)S(1)} all-reduce(bf16[1280]{0:T(1024)(128)(2,1)S(1)} %dynamic-update-slice), channel_id=1, replica_groups=mesh['grp'=8,'mem'=4] {'mem'}, use_global_device_ids=true, to_apply=%add | all-reduce | flops 1280 | bytes 5120
  55.6 6.2 %all-gather.2.cloned.1.call-done = bf16[1280,1024]{1,0:T(8,128)(2,1)} async-done(((bf16[320,1024]{1,0:T(8,128)(2,1)}), bf16[1280,1024]{1,0:T(8,128)(2,1)}) %all-gather.2.cloned.1.call-update) | async-done | bytes 2621456 | tf_op jit(solution)/shard_map/all_gather | solution.py:84
  61.8 3.7 %fusion.18 = (f32[320]{0:T(512)S(1)}, bf16[320,1280]{1,0:T(8,128)(2,1)S(1)}) fusion(bf16[320,1024]{1,0:T(8,128)(2,1)} %bitcast.28, bf16[1280,1024]{1,0:T(8,128)(2,1)} %all-gather.2.cloned.1.call-done, s32[320]{0:T(512)S(1)} %iota_add_fusion, pred[320]{0:T(512)(128)(4,1)S(1)} %broadcast_compare_fusion, bf16[1280]{0:T(1024)(128)(2,1)S(1)} %all-reduce, ...), kind=kOutput, calls=%fused_computation.55 | convolution fusion | flops 843775680 | bytes 4102080 | tf_op jit(solution)/shard_map/dot_general | solution.py:27
  65.5 1.0 %divide_convert_fusion = bf16[320,1024]{1,0:T(8,128)(2,1)S(1)} fusion(bf16[1280,1024]{1,0:T(8,128)(2,1)S(1)} %copy-done.2, bf16[320,1024]{1,0:T(8,128)(2,1)S(1)} %bitcast.29, bf16[320,1280]{1,0:T(8,128)(2,1)S(1)} %get-tuple-element.15, f32[320]{0:T(512)S(1)} %get-tuple-element.11), kind=kOutput, calls=%fused_computation.16 | convolution fusion | flops 840171520 | bytes 4752640 | tf_op jit(solution)/shard_map/dot_general | solution.py:40
  66.6 0.3 fusion.7
  66.9 4.3 %collective-permute-start = (bf16[1,40,1024]{2,1,0:T(8,128)(2,1)S(1)}, bf16[1,40,1024]{2,1,0:T(8,128)(2,1)S(1)}, u32[]{:S(2)}, u32[]{:S(2)}) collective-permute-start(bf16[1,40,1024]{2,1,0:T(8,128)(2,1)S(1)} %get-tuple-element.9), channel_id=1, source_target_pairs={{0,28},{4,0},{8,4},{12,8},{16,12},{20,16},{24,20},{28,24},{1,29},{... | collective-permute-start | bytes 245768 | tf_op jit(solution)/shard_map/ppermute | solution.py:103
  71.2 0.7 convert_element_type.50
  71.8 3.3 %all-to-all-start.2 = ((bf16[8,1,40]{2,1,0:T(2,128)(2,1)}), bf16[8,1,40]{2,1,0:T(2,128)(2,1)S(1)}, u32[]{:S(2)}, u32[]{:S(2)}) async-start(bf16[8,1,40]{2,1,0:T(2,128)(2,1)} %convert_element_type.50), calls=%async_computation.2 | async-start | bytes 8192 | tf_op jit(solution)/shard_map/all_to_all | solution.py:110
  75.2 3.7 %collective-permute-start.1 = (bf16[1,40,1024]{2,1,0:T(8,128)(2,1)S(1)}, bf16[1,40,1024]{2,1,0:T(8,128)(2,1)S(1)}, u32[]{:S(2)}, u32[]{:S(2)}) collective-permute-start(bf16[1,40,1024]{2,1,0:T(8,128)(2,1)S(1)} %get-tuple-element.8), channel_id=1, source_target_pairs={{0,24},{4,28},{8,0},{12,4},{16,8},{20,12},{24,16},{28,20},{1,25},{... | collective-permute-start | bytes 245768 | tf_op jit(solution)/shard_map/ppermute | solution.py:103
  78.9 0.5 collective-permute-start.2
  79.5 3.3 %collective-permute-start.3 = (bf16[1,40,1024]{2,1,0:T(8,128)(2,1)S(1)}, bf16[1,40,1024]{2,1,0:T(8,128)(2,1)S(1)}, u32[]{:S(2)}, u32[]{:S(2)}) collective-permute-start(bf16[1,40,1024]{2,1,0:T(8,128)(2,1)S(1)} %get-tuple-element.6), channel_id=1, source_target_pairs={{0,16},{4,20},{8,24},{12,28},{16,0},{20,4},{24,8},{28,12},{1,17},{... | collective-permute-start | bytes 245768 | tf_op jit(solution)/shard_map/ppermute | solution.py:103
  82.7 0.0 collective-permute-start.4
  82.7 0.0 all-to-all-done.2
  82.8 0.1 reshape.103
  82.9 2.5 %gather_fusion.1 = bf16[256]{0:T(256)(128)(2,1)} fusion(bf16[320]{0:T(512)(128)(2,1)S(1)} %reshape.103, s32[1024]{0:T(1024)S(1)} %pad_clamp_fusion), kind=kCustom, calls=%fused_computation.1 | custom fusion | bytes 2048 | tf_op jit(solution)/shard_map/gather | solution.py:113
  85.3 0.0 collective-permute-done
  85.3 1.1 %collective-permute-start.5 = (bf16[1,40,1024]{2,1,0:T(8,128)(2,1)S(1)}, bf16[1,40,1024]{2,1,0:T(8,128)(2,1)S(1)}, u32[]{:S(2)}, u32[]{:S(2)}) collective-permute-start(bf16[1,40,1024]{2,1,0:T(8,128)(2,1)S(1)} %get-tuple-element.4), channel_id=1, source_target_pairs={{0,8},{4,12},{8,16},{12,20},{16,24},{20,28},{24,0},{28,4},{1,9},{5... | collective-permute-start | bytes 245768 | tf_op jit(solution)/shard_map/ppermute | solution.py:103
  86.4 0.0 collective-permute-done.1
  86.4 1.5 %collective-permute-start.6 = (bf16[1,40,1024]{2,1,0:T(8,128)(2,1)S(1)}, bf16[1,40,1024]{2,1,0:T(8,128)(2,1)S(1)}, u32[]{:S(2)}, u32[]{:S(2)}) collective-permute-start(bf16[1,40,1024]{2,1,0:T(8,128)(2,1)S(1)} %get-tuple-element.3), channel_id=1, source_target_pairs={{0,4},{4,8},{8,12},{12,16},{16,20},{20,24},{24,28},{28,0},{1,5},{5... | collective-permute-start | bytes 245768 | tf_op jit(solution)/shard_map/ppermute | solution.py:103
  88.0 0.0 collective-permute-done.2
  88.0 4.3 %collective-permute-done.3 = bf16[1,40,1024]{2,1,0:T(8,128)(2,1)S(1)} collective-permute-done((bf16[1,40,1024]{2,1,0:T(8,128)(2,1)S(1)}, bf16[1,40,1024]{2,1,0:T(8,128)(2,1)S(1)}, u32[]{:S(2)}, u32[]{:S(2)}) %collective-permute-start.3) | collective-permute-done | bytes 81952 | tf_op jit(solution)/shard_map/ppermute | solution.py:103
  92.3 1.5 %collective-permute-done.4 = bf16[1,40,1024]{2,1,0:T(8,128)(2,1)S(1)} collective-permute-done((bf16[1,40,1024]{2,1,0:T(8,128)(2,1)S(1)}, bf16[1,40,1024]{2,1,0:T(8,128)(2,1)S(1)}, u32[]{:S(2)}, u32[]{:S(2)}) %collective-permute-start.4) | collective-permute-done | bytes 81952 | tf_op jit(solution)/shard_map/ppermute | solution.py:103
  93.8 0.0 collective-permute-done.5
  93.8 0.0 collective-permute-done.6
  93.9 0.3 fusion.6
  94.1 2.0 %gather_fusion = bf16[256,1024]{1,0:T(8,128)(2,1)} fusion(bf16[320,1024]{1,0:T(8,128)(2,1)S(1)} %bitcast.24, s32[1024]{0:T(1024)S(1)} %pad_clamp_fusion), kind=kCustom, calls=%fused_computation | custom fusion | bytes 1049600 | tf_op jit(solution)/shard_map/gather | solution.py:112
  (26 shorter events, 0.2 us)
Async XLA Ops:
  7.2 2.9 %copy-start.1 = (bf16[256,1024]{1,0:T(8,128)(2,1)S(1)}, bf16[256,1024]{1,0:T(8,128)(2,1)}, u32[]{:S(2)}) copy-start(bf16[256,1024]{1,0:T(8,128)(2,1)} %param.5) | copy-start | bytes 1572868
  7.2 54.6 %all-gather.2.cloned.1.call-start = ((), (), s32[]{:S(2)}) async-start(), calls=%async_computation.3 | async-start | bytes 3276800 | tf_op jit(solution)/shard_map/all_gather | solution.py:84
  10.4 32.4 %copy-start.3 = (u32[32]{0:T(128)S(1)}, u32[32]{0:T(128)}, u32[]{:S(2)}) copy-start(u32[32]{0:T(128)} %constant.79) | copy-start | bytes 388
  39.4 9.6 %all-to-all-start.1 = ((bf16[8,1,40]{2,1,0:T(2,128)(2,1)}), bf16[8,1,40]{2,1,0:T(2,128)(2,1)S(1)}, u32[]{:S(2)}, u32[]{:S(2)}) async-start(bf16[8,1,40]{2,1,0:T(2,128)(2,1)} %all_to_all.17), calls=%async_computation.1 | async-start | bytes 8192 | tf_op jit(solution)/shard_map/all_to_all | solution.py:74
  55.6 9.9 %copy-start = (bf16[8,40,1024]{2,1,0:T(8,128)(2,1)S(1)}, bf16[8,40,1024]{2,1,0:T(8,128)(2,1)}, u32[]{:S(2)}) copy-start(bf16[8,40,1024]{2,1,0:T(8,128)(2,1)} %all_to_all.21) | copy-start | bytes 1966084
  61.8 3.7 %copy-start.2 = (bf16[1280,1024]{1,0:T(8,128)(2,1)S(1)}, bf16[1280,1024]{1,0:T(8,128)(2,1)}, u32[]{:S(2)}) copy-start(bf16[1280,1024]{1,0:T(8,128)(2,1)} %all-gather.2.cloned.1.call-done) | copy-start | bytes 7864324
  66.9 18.5 %collective-permute-start = (bf16[1,40,1024]{2,1,0:T(8,128)(2,1)S(1)}, bf16[1,40,1024]{2,1,0:T(8,128)(2,1)S(1)}, u32[]{:S(2)}, u32[]{:S(2)}) collective-permute-start(bf16[1,40,1024]{2,1,0:T(8,128)(2,1)S(1)} %get-tuple-element.9), channel_id=1, source_target_pairs={{0,28},{4,0},{8,4},{12,8},{16,12},{20,16},{24,20},{28,24},{1,29},{... | collective-permute-start | bytes 245768 | tf_op jit(solution)/shard_map/ppermute | solution.py:103
  71.8 10.9 %all-to-all-start.2 = ((bf16[8,1,40]{2,1,0:T(2,128)(2,1)}), bf16[8,1,40]{2,1,0:T(2,128)(2,1)S(1)}, u32[]{:S(2)}, u32[]{:S(2)}) async-start(bf16[8,1,40]{2,1,0:T(2,128)(2,1)} %convert_element_type.50), calls=%async_computation.2 | async-start | bytes 8192 | tf_op jit(solution)/shard_map/all_to_all | solution.py:110
  75.2 11.3 %collective-permute-start.1 = (bf16[1,40,1024]{2,1,0:T(8,128)(2,1)S(1)}, bf16[1,40,1024]{2,1,0:T(8,128)(2,1)S(1)}, u32[]{:S(2)}, u32[]{:S(2)}) collective-permute-start(bf16[1,40,1024]{2,1,0:T(8,128)(2,1)S(1)} %get-tuple-element.8), channel_id=1, source_target_pairs={{0,24},{4,28},{8,0},{12,4},{16,8},{20,12},{24,16},{28,20},{1,25},{... | collective-permute-start | bytes 245768 | tf_op jit(solution)/shard_map/ppermute | solution.py:103
  78.9 9.1 %collective-permute-start.2 = (bf16[1,40,1024]{2,1,0:T(8,128)(2,1)S(1)}, bf16[1,40,1024]{2,1,0:T(8,128)(2,1)S(1)}, u32[]{:S(2)}, u32[]{:S(2)}) collective-permute-start(bf16[1,40,1024]{2,1,0:T(8,128)(2,1)S(1)} %get-tuple-element.7), channel_id=1, source_target_pairs={{0,20},{4,24},{8,28},{12,0},{16,4},{20,8},{24,12},{28,16},{1,21},{... | collective-permute-start | bytes 245768 | tf_op jit(solution)/shard_map/ppermute | solution.py:103
  79.5 12.8 %collective-permute-start.3 = (bf16[1,40,1024]{2,1,0:T(8,128)(2,1)S(1)}, bf16[1,40,1024]{2,1,0:T(8,128)(2,1)S(1)}, u32[]{:S(2)}, u32[]{:S(2)}) collective-permute-start(bf16[1,40,1024]{2,1,0:T(8,128)(2,1)S(1)} %get-tuple-element.6), channel_id=1, source_target_pairs={{0,16},{4,20},{8,24},{12,28},{16,0},{20,4},{24,8},{28,12},{1,17},{... | collective-permute-start | bytes 245768 | tf_op jit(solution)/shard_map/ppermute | solution.py:103
  82.7 11.1 %collective-permute-start.4 = (bf16[1,40,1024]{2,1,0:T(8,128)(2,1)S(1)}, bf16[1,40,1024]{2,1,0:T(8,128)(2,1)S(1)}, u32[]{:S(2)}, u32[]{:S(2)}) collective-permute-start(bf16[1,40,1024]{2,1,0:T(8,128)(2,1)S(1)} %get-tuple-element.5), channel_id=1, source_target_pairs={{0,12},{4,16},{8,20},{12,24},{16,28},{20,0},{24,4},{28,8},{1,13},{... | collective-permute-start | bytes 245768 | tf_op jit(solution)/shard_map/ppermute | solution.py:103
  85.3 8.5 %collective-permute-start.5 = (bf16[1,40,1024]{2,1,0:T(8,128)(2,1)S(1)}, bf16[1,40,1024]{2,1,0:T(8,128)(2,1)S(1)}, u32[]{:S(2)}, u32[]{:S(2)}) collective-permute-start(bf16[1,40,1024]{2,1,0:T(8,128)(2,1)S(1)} %get-tuple-element.4), channel_id=1, source_target_pairs={{0,8},{4,12},{8,16},{12,20},{16,24},{20,28},{24,0},{28,4},{1,9},{5... | collective-permute-start | bytes 245768 | tf_op jit(solution)/shard_map/ppermute | solution.py:103
  86.4 7.4 %collective-permute-start.6 = (bf16[1,40,1024]{2,1,0:T(8,128)(2,1)S(1)}, bf16[1,40,1024]{2,1,0:T(8,128)(2,1)S(1)}, u32[]{:S(2)}, u32[]{:S(2)}) collective-permute-start(bf16[1,40,1024]{2,1,0:T(8,128)(2,1)S(1)} %get-tuple-element.3), channel_id=1, source_target_pairs={{0,4},{4,8},{8,12},{12,16},{16,20},{20,24},{24,28},{28,0},{1,5},{5... | collective-permute-start | bytes 245768 | tf_op jit(solution)/shard_map/ppermute | solution.py:103
Sparse Core Ops, SparseCore 0:
  37.4 24.3 all-gather.1
